TPU v7x, 1024 devices: a whole 4x8x16 slice. The times are simulated.
1024 devices in a mesh: row: 256 (over y, z, core), col: 4 (over x).
Axes of the slice: x: 4, y: 8, z: 16, core: 2. Of those that a mesh axis runs over, the one named last changes fastest.
Arguments:
- weight: float32 [25600, 5120], P('row', 'col'), may hold values from -6 to 6
- grad: float32 [25600, 5120], P('row', 'col'), may hold values from -6 to 6
- momentum: float32 [25600, 5120], P('row', 'col'), may hold values from -90 to 90
- right_factor: bfloat16 [5120, 256], P('col'), may hold values from -0.078125 to 0.078125
Outputs:
- new_weight: float32 [25600, 5120], P('row', 'col')
- new_momentum: float32 [25600, 5120], P('row', 'col')
- new_right: bfloat16 [5120, 256], P(('col', 'row'))
All inputs are finite; a program needn't handle non-finite values.
Results may differ from a plain program's by a relative error of at most 0.0023.
Values sent between devices are 32-bit elements; how exact they have to be, the bound alone decides.
A program may use at most 32 MiB of HBM per device.

v0:
```python
import jax
import jax.numpy as jnp
from jax import lax
from jax.sharding import PartitionSpec as P

M = 25600
N = 5120
R = 256


feedback_share = 0.05
decay_keep = 0.999
step_rate = 0.5
epsilon = 1e-06


def on_device(weight, grad, momentum, right_factor):
    highest = lax.Precision.HIGHEST
    buffer = momentum + grad
    partial_value = jnp.dot(buffer, right_factor.astype(jnp.float32), precision=highest)
    proj = lax.psum(partial_value, "col")
    gram = lax.psum(jnp.dot(proj.T, proj, precision=highest), "row")
    factor = jnp.linalg.cholesky(gram)
    ortho = lax.linalg.triangular_solve(factor, proj, left_side=False, lower=True, transpose_a=True)
    scale = (M * N / R) ** 0.5
    right_rows = lax.psum_scatter(
        jnp.dot(buffer.T, ortho, precision=highest), "row", scatter_dimension=0, tiled=True
    )
    squares = jnp.sum(right_rows * right_rows, axis=0)
    total = lax.psum(squares, ("row", "col"))
    inverse = 1.0 / jnp.sqrt(total + epsilon)
    new_right = (right_rows * inverse).astype(jnp.bfloat16)
    scaled = ortho * inverse
    piece = lax.all_gather(right_rows, "row", axis=0, tiled=True)
    feedback = jnp.dot(ortho, piece.T, precision=highest)
    update = jnp.dot(scaled, piece.T, precision=highest)
    both = jnp.stack([feedback, update])
    feedback = both[0]
    update = both[1]
    new_momentum = buffer - feedback_share * feedback
    new_weight = decay_keep * weight - step_rate * scale * update
    return (new_weight, new_momentum, new_right)


def solution(mesh):
    placed = (P("row", "col"), P("row", "col"), P("row", "col"), P("col", None))
    return jax.shard_map(
        on_device,
        mesh=mesh,
        in_specs=placed,
        out_specs=(P("row", "col"), P("row", "col"), P(("col", "row"), None)),
        check_vma=False,
    )
```

profile of v0, /device:TPU:1, one launch (start us, length us, event | category | flops | bytes accessed | tf_op | source)
XLA Modules:
  0.0 1111.3 jit_solution(5895738284810945051)
XLA Ops:
  7.2 0.0 copy-start
  7.2 0.0 all-reduce.6.cloned.1.call-start
  7.2 1.3 add.39
  8.5 0.0 copy-done
  8.6 1.1 fusion.17
  9.7 0.0 all-reduce.6.cloned.1.call-update
  9.7 0.0 all-reduce.8.cloned.1.call-start
  9.7 69.7 %all-reduce.6.cloned.1.call-done = f32[100,256]{1,0:T(8,128)} async-done(((f32[100,256]{1,0:T(8,128)}), f32[100,256]{1,0:T(8,128)}) %all-reduce.6.cloned.1.call-update) | async-done | bytes 102416 | tf_op jit(solution)/shard_map/psum | solution.py:21
  79.4 2.1 fusion.18
  81.5 0.0 all-reduce.8.cloned.1.call-update
  81.6 0.0 all-reduce.10.cloned.1.call-start
  81.6 345.9 %all-reduce.8.cloned.1.call-done = f32[256,256]{0,1:T(8,128)} async-done(((f32[256,256]{0,1:T(8,128)}), f32[256,256]{0,1:T(8,128)}) %all-reduce.8.cloned.1.call-update) | async-done | bytes 262160 | tf_op jit(solution)/shard_map/psum | solution.py:22
  427.5 1.1 copy.12
  428.6 1.0 fusion.2
  429.6 0.0 copy-start.1
  429.6 11.7 %cholesky.50 = f32[128,128]{1,0:T(8,128)S(1)} custom-call(f32[128,128]{1,0:T(8,128)S(1)} %cholesky.118), custom_call_target="Cholesky" | custom-call | tf_op jit(solution)/shard_map/jit(cholesky)/cholesky | solution.py:23
  441.3 9.8 custom-call.14
  451.2 0.2 constant_dynamic-update-slice_fusion.1
  451.4 0.3 convolution_subtract_fusion
  451.7 11.7 %cholesky.105 = f32[128,128]{1,0:T(8,128)S(1)} custom-call(f32[128,128]{1,0:T(8,128)S(1)} %convolution_subtract_fusion), custom_call_target="Cholesky" | custom-call | tf_op jit(solution)/shard_map/jit(cholesky)/cholesky | solution.py:23
  463.4 0.6 compare_reduce_fusion
  465.4 0.1 triangular_solve.58
  465.5 4.1 while.1
  465.6 0.6 fusion.31
  466.2 1.4 bitcast_dynamic-update-slice_fusion.2
  467.6 0.6 fusion.31
  468.2 1.4 bitcast_dynamic-update-slice_fusion.2
  469.6 19.7 %custom-call.15 = f32[2,128,128]{1,2,0:T(8,128)S(1)} custom-call(f32[2,128,128]{2,1,0:T(8,128)S(1)} %get-tuple-element.10), custom_call_target="InvertDiagBlocksLowerTriangular" | custom-call | tf_op jit(solution)/shard_map/triangular_solve | solution.py:24
  489.3 0.0 copy-done.1
  489.3 0.2 fusion.7
  489.5 0.3 convolution_subtract_fusion.1
  489.8 0.2 fusion.5
  490.1 2.3 fusion.4
  492.4 0.0 all-reduce.10.cloned.1.call-update
  492.4 0.0 all-gather.3.cloned.1.call-start
  492.4 1.3 dynamic-slice.3
  494.4 350.2 %all-reduce.10.cloned.1.call-done = f32[1280,256]{1,0:T(8,128)} async-done(((f32[1280,256]{1,0:T(8,128)}), f32[1280,256]{1,0:T(8,128)}) %all-reduce.10.cloned.1.call-update) | async-done | bytes 1310736
  844.6 0.7 multiply_reduce_fusion
  845.3 120.2 %psum.23 = f32[256]{0:T(256)S(1)} all-reduce(f32[256]{0:T(256)S(1)} %multiply_reduce_fusion), channel_id=1, replica_groups=mesh['row'=256,'col'=4] {'row','col'}, use_global_device_ids=true, to_apply=%region_8.9 | all-reduce | flops 256 | bytes 2048 | tf_op jit(solution)/shard_map/psum | solution.py:30
  965.5 1.3 multiply_convert_fusion
  966.8 0.0 all-gather.3.cloned.1.call-update
  966.9 131.9 %all-gather.3.cloned.1.call-done = f32[256,5,256]{2,1,0:T(8,128)} async-done(((f32[1,5,256]{2,1,0:T(8,128)}), f32[256,5,256]{2,1,0:T(8,128)}) %all-gather.3.cloned.1.call-update) | async-done | bytes 1310736 | tf_op jit(solution)/shard_map/all_gather | solution.py:34
  1098.7 1.6 reshape.44
  1100.4 0.0 copy-start.2
  1100.4 2.2 fusion.1
  1102.6 0.0 copy-done.2
  1102.6 2.2 fusion
  (10 shorter events, 0.2 us)
Async XLA Ops:
  7.2 1.4 copy-start
  7.2 72.3 %all-reduce.6.cloned.1.call-start = ((), (), s32[]{:S(2)}) async-start(), calls=%async_computation | async-start | bytes 212992 | tf_op jit(solution)/shard_map/psum | solution.py:21
  9.7 417.8 %all-reduce.8.cloned.1.call-start = ((), (), s32[]{:S(2)}) async-start(), calls=%async_computation.1 | async-start | bytes 524288 | tf_op jit(solution)/shard_map/psum | solution.py:22
  81.6 763.0 %all-reduce.10.cloned.1.call-start = ((), (), s32[]{:S(2)}) async-start(), calls=%async_computation.3 | async-start | bytes 2621440
  429.6 59.7 %copy-start.1 = (f32[100,256]{1,0:T(8,128)S(1)}, f32[100,256]{1,0:T(8,128)}, u32[]{:S(2)}) copy-start(f32[100,256]{1,0:T(8,128)} %all-reduce.6.cloned.1.call-done) | copy-start | bytes 307204
  492.4 606.3 %all-gather.3.cloned.1.call-start = ((), (), s32[]{:S(2)}) async-start(), calls=%async_computation.2 | async-start | bytes 2105344 | tf_op jit(solution)/shard_map/all_gather | solution.py:34
  1100.4 2.2 copy-start.2
Sparse Core Ops, SparseCore 0:
  10.9 68.5 all-reduce.5
  83.5 343.9 all-reduce.7
  492.5 352.0 all-reduce.9
  967.0 131.6 all-gather.2
where the time goes:
time: 1110 us
  waiting for transfers between devices  898 us (81%)
  blocking collectives  120 us (11%)
  other arithmetic  58 us (5%)
  between operations  15.9 us (1%)
  matrix products  11.1 us (1%)
    unnamed x5, waiting for transfers between devices  350 us
    psum x1, waiting for transfers between devices, on_device(): gram = lax.psum(jnp.dot(proj.T, proj, precision=highest), 'row')  346 us
    all_gather x1, waiting for transfers between devices, on_device(): piece = lax.all_gather(right_rows, 'row', axis=0, tiled=True)  132 us
    psum x1, blocking collectives, on_device(): total = lax.psum(squares, ('row', 'col'))  120 us
    psum x1, waiting for transfers between devices, on_device(): proj = lax.psum(partial_value, 'col')  69.7 us
    another operation x6, other arithmetic, on_device(): factor = jnp.linalg.cholesky(gram)  34 us
  transfers between devices with their start and end apart: 4, of which 4 were waited for; matrix products, arithmetic and copies ran while one was open for 0% of the time, Pallas kernels for 0%

commit v1 on v0

v1 whole, which is shorter than its diff:
```python
import functools

import jax
import jax.numpy as jnp
from jax import lax
from jax.experimental import pallas as pl
from jax.experimental.pallas import tpu as pltpu
from jax.sharding import PartitionSpec as P

M = 25600
N = 5120
R = 256

feedback_share = 0.05
decay_keep = 0.999
step_rate = 0.5
epsilon = 1e-06

CORES = 2
ZL = 4
HALF = 128
F32 = jnp.float32
BF16 = jnp.bfloat16
NN = (((1,), (0,)), ((), ()))
NT = (((1,), (1,)), ((), ()))
TN = (((0,), (0,)), ((), ()))


def exact(a, b, dims):
    return lax.dot_general(a, b, dims, precision=lax.Precision.HIGHEST, preferred_element_type=F32)


def single(a, b, dims):
    return lax.dot_general(a, b, dims, preferred_element_type=F32)


def split(a):
    high = a.astype(BF16)
    return high, (a - high.astype(F32)).astype(BF16)


def triple(a, b, dims):
    ah, al = split(a)
    bh, bl = split(b)
    return single(ah, bh, dims) + (single(ah, bl, dims) + single(al, bh, dims))


def thirds(a):
    high = a.astype(BF16).astype(F32)
    rest = a - high
    middle = rest.astype(BF16).astype(F32)
    return high, middle, rest - middle


def invert_factor(work):
    lane = lax.broadcasted_iota(jnp.int32, (8, HALF), 1)
    sub = lax.broadcasted_iota(jnp.int32, (8, HALF), 0)

    def group(g, carry):
        base = pl.multiple_of(g * 8, 8)
        ra = work[pl.ds(base, 8), 0:HALF]
        rb = work[pl.ds(base, 8), HALF:]
        columns = [
            jnp.broadcast_to(
                jnp.sum(jnp.where(lane == base + i, ra, 0.0), axis=1, keepdims=True), (8, HALF)
            )
            for i in range(8)
        ]
        for i in range(8):
            pivot = jnp.broadcast_to(columns[i][i : i + 1, :], (8, HALF))
            s = lax.rsqrt(pivot)
            s = s * (1.5 - 0.5 * pivot * s * s)
            scaled = columns[i] * s
            below = jnp.where(sub > i, scaled, 0.0)
            for j in range(i + 1, 8):
                columns[j] = columns[j] - below * jnp.broadcast_to(scaled[j : j + 1, :], (8, HALF))
            pa = jnp.broadcast_to(ra[i : i + 1, :], (8, HALF)) * s
            pb = jnp.broadcast_to(rb[i : i + 1, :], (8, HALF)) * s
            ra = jnp.where(sub == i, pa, ra - below * pa)
            rb = jnp.where(sub == i, pb, rb - below * pb)
        work[pl.ds(base, 8), 0:HALF] = ra
        work[pl.ds(base, 8), HALF:] = rb
        masked = jnp.where(lane >= base + 8, ra, 0.0)
        lh, lm, ll = thirds(masked)
        full = jnp.concatenate([ra, rb], axis=1)
        rh, rm, rl = thirds(full)
        left = jnp.concatenate([lh, lh, lm, lh, ll, lm], axis=0).astype(BF16)
        right = jnp.concatenate([rh, rm, rh, rl, rh, rm], axis=0).astype(BF16)
        work[...] = work[...] - single(left, right, TN)
        return carry

    lax.fori_loop(0, HALF // 8, group, 0)


def kernel(
    dims, weight, grad, momentum, factor, new_weight, new_momentum, new_right,
    buf, part, both, rx, wt, cw, accw, yw, ysum, zw, hw, full,
    gp, gc, ga, gy, gz, gh, gfin, work, inv, rt, n0, n1, n2, n3, ssem, rsem,
):
    Y, ZH = dims
    rows = weight.shape[0]
    padded = buf.shape[0]
    span = weight.shape[1] // 2
    ry = HALF // Y
    rc = ry // 2
    rg = 64 // Y
    Z = ZH * ZL
    r = lax.axis_index("row")
    c = lax.axis_index("col")
    core = lax.rem(r, CORES)
    z = lax.rem(r // CORES, Z)
    y = r // (CORES * Z)
    zl = lax.rem(z, ZL)
    zh = z // ZL

    def at(y, z, core, c):
        return {"row": (y * Z + z) * CORES + core, "col": c}

    near = at(y, z, core, c + 1 - 2 * lax.rem(c, 2))
    far = at(y, z, core, 3 - c)
    twin = at(y, z, 1 - core, c)
    ys = [lax.rem(y + d, Y) for d in range(1, Y)]
    zls = [lax.rem(zl + d, ZL) for d in range(1, ZL)]
    zhs = [lax.rem(zh + d, ZH) for d in range(1, ZH)]
    ydev = [at(q, z, core, c) for q in ys]
    zldev = [at(y, zh * ZL + q, core, c) for q in zls]
    zhdev = [at(y, q * ZL + zl, core, c) for q in zhs]

    count = [0]

    def send(src, dst, device):
        k = count[0]
        count[0] += 1
        copy = pltpu.make_async_remote_copy(
            src_ref=src, dst_ref=dst, send_sem=ssem.at[k], recv_sem=rsem.at[k],
            device_id=device, device_id_type=pl.DeviceIdType.MESH,
        )
        copy.start()
        sent.append(copy)
        return copy

    sent = []

    def arrive(copies):
        for copy in copies:
            copy.wait_recv()

    barrier = pltpu.get_barrier_semaphore()
    peers = [near, far, twin] + ydev + zldev + zhdev
    for device in peers:
        pl.semaphore_signal(barrier, inc=1, device_id=device, device_id_type=pl.DeviceIdType.MESH)

    buf[0:rows, :] = momentum[...] + grad[...]
    buf[rows:padded, :] = jnp.zeros((padded - rows, 2 * span), F32)
    value = buf[...]
    bh = value.astype(BF16)
    rest = value - bh.astype(F32)
    bm = rest.astype(BF16)
    bl = (rest - bm.astype(F32)).astype(BF16)
    fr = factor[...]
    partial_value = single(bh, fr, NN) + (single(bm, fr, NN) + single(bl, fr, NN))
    part[0] = partial_value[:, 0:HALF]
    part[1] = partial_value[:, HALF:]
    pl.semaphore_wait(barrier, len(peers))

    one = [send(part.at[0], rx.at[0], near), send(part.at[1], rx.at[1], far)]
    arrive(one)
    both[...] = part[...] + rx[0:2]
    two = [send(both.at[0], rx.at[2], far), send(both.at[1], rx.at[3], near)]
    arrive(two)
    part0 = both[0] + rx[2]
    part1 = both[1] + rx[3]
    proj = jnp.concatenate([part0, part1], axis=1)

    gram = exact(proj, proj, TN)
    gp[0] = gram[:, 0:HALF]
    gp[1] = gram[:, HALF:]
    quarter = pl.multiple_of(c * 64, 64)
    gcopy = send(gp.at[1 - core, pl.ds(quarter, 64)], gc, twin)
    ph, pm = split(proj)
    for h in range(2):
        b_h, b_l = split(buf[:, span * h : span * (h + 1)])
        wt[h] = single(ph, b_h, TN) + (single(ph, b_l, TN) + single(pm, b_h, TN))
    other = pl.multiple_of((1 - core) * HALF, HALF)
    mine = pl.multiple_of(core * HALF, HALF)
    wcopy = send(wt.at[:, pl.ds(other, HALF)], cw, twin)

    arrive([gcopy])
    ga[...] = gp[core, pl.ds(quarter, 64), :] + gc[...]
    gcopies = [
        send(ga.at[pl.ds(pl.multiple_of(q * rg, 8), rg)], gy.at[d], ydev[d]) for d, q in enumerate(ys)
    ]
    arrive([wcopy])
    accw[...] = wt[:, pl.ds(mine, HALF), :] + cw[...]
    wcopies = [
        send(accw.at[:, pl.ds(pl.multiple_of(q * ry, ry), ry)], yw.at[d], ydev[d])
        for d, q in enumerate(ys)
    ]
    arrive(gcopies)
    tile = ga[pl.ds(pl.multiple_of(y * rg, 8), rg), :]
    for d in range(Y - 1):
        tile = tile + gy[d]
    gz[zl] = tile
    gcopies = [send(gz.at[zl], gz.at[zl], device) for device in zldev]
    arrive(gcopies)
    gh[zh] = (gz[0] + gz[1]) + (gz[2] + gz[3])
    gcopies = [send(gh.at[zh], gh.at[zh], device) for device in zhdev]
    arrive(gcopies)
    tile = gh[0]
    for q in range(1, ZH):
        tile = tile + gh[q]
    spot = pl.multiple_of(c * 64 + y * rg, 8)
    gfin[core, pl.ds(spot, rg), :] = tile
    gcopies = [
        send(gfin.at[core, pl.ds(spot, rg)], gfin.at[core, pl.ds(spot, rg)], device) for device in ydev
    ]

    arrive(wcopies)
    block = accw[:, pl.ds(pl.multiple_of(y * ry, ry), ry), :]
    for d in range(Y - 1):
        block = block + yw[d]
    ysum[...] = block
    wcopies = [
        send(
            ysum.at[lax.rem(q, 2), pl.ds(pl.multiple_of((q // 2) * rc, rc), rc)], zw.at[d], zldev[d]
        )
        for d, q in enumerate(zls)
    ]
    arrive(gcopies)
    gcopy = send(
        gfin.at[core, pl.ds(quarter, 64)], gfin.at[core, pl.ds(quarter, 64)], twin
    )
    arrive([gcopy])
    gcopy = send(gfin.at[:, pl.ds(quarter, 64)], gfin.at[:, pl.ds(quarter, 64)], near)
    arrive(wcopies)
    piece = ysum[lax.rem(zl, 2), pl.ds(pl.multiple_of((zl // 2) * rc, rc), rc), :]
    for d in range(ZL - 1):
        piece = piece + zw[d]
    hw[zh] = piece
    wcopies = [send(hw.at[zh], hw.at[zh], device) for device in zhdev]
    arrive([gcopy])
    pair = pl.multiple_of((c // 2) * HALF, HALF)
    gcopy = send(gfin.at[:, pl.ds(pair, HALF)], gfin.at[:, pl.ds(pair, HALF)], far)
    arrive(wcopies)
    piece = hw[0]
    for q in range(1, ZH):
        piece = piece + hw[q]
    spot = pl.multiple_of(core * HALF + y * ry + (zl // 2) * rc, rc)
    hz = lax.rem(zl, 2)
    full[hz, pl.ds(spot, rc), :] = piece
    wcopies = [
        send(full.at[hz, pl.ds(spot, rc)], full.at[hz, pl.ds(spot, rc)], device) for device in zldev
    ]
    arrive(wcopies)
    strip = pl.multiple_of(core * HALF + y * ry, ry)
    wcopies = [
        send(full.at[:, pl.ds(strip, ry)], full.at[:, pl.ds(strip, ry)], device) for device in ydev
    ]
    arrive([gcopy])

    eye = jnp.where(
        lax.broadcasted_iota(jnp.int32, (HALF, HALF), 0)
        == lax.broadcasted_iota(jnp.int32, (HALF, HALF), 1),
        1.0,
        0.0,
    ).astype(F32)
    work[:, 0:HALF] = gfin[0, 0:HALF, :]
    work[:, HALF:] = eye
    invert_factor(work)
    arrive(wcopies)
    wcopy = send(full.at[:, pl.ds(mine, HALF)], full.at[:, pl.ds(mine, HALF)], twin)
    top = work[:, HALF:]
    low = exact(gfin[0, HALF:, :], top, NT)
    inv[0:HALF, 0:HALF] = top
    inv[0:HALF, HALF:] = jnp.zeros((HALF, HALF), F32)
    work[:, 0:HALF] = gfin[1, HALF:, :] - exact(low, low, NT)
    work[:, HALF:] = eye
    cross = exact(low, top, NN)
    invert_factor(work)
    last = work[:, HALF:]
    inv[HALF:, 0:HALF] = -exact(last, cross, NN)
    inv[HALF:, HALF:] = last

    whole = inv[...]
    ortho = triple(proj, whole, NT)
    arrive([wcopy])
    ones = jnp.ones((8, span), F32)
    norms = jnp.zeros((8, R), F32)
    for h in range(2):
        value = triple(whole, full[h], NN)
        rt[h] = value
        norms = norms + exact(ones, value * value, NT)
    n0[...] = norms
    copy = send(n0, n1, near)
    copies = [copy]
    for h in range(2):
        lanes = slice(span * h, span * (h + 1))
        feedback = triple(ortho, rt[h], NN)
        new_momentum[:, lanes] = buf[0:rows, lanes] - feedback_share * feedback[0:rows]
    picked = jnp.zeros((8, R), F32)
    for h in range(2):
        want = 5 * r + lax.broadcasted_iota(jnp.int32, (8, span), 0)
        have = span * h + lax.broadcasted_iota(jnp.int32, (8, span), 1)
        chosen = jnp.where(want == have, 1.0, 0.0).astype(F32)
        picked = picked + exact(chosen, rt[h], NT)
    arrive(copies)
    n2[...] = n0[...] + n1[...]
    copies = [send(n2, n3, far)]
    arrive(copies)
    inverse = 1.0 / jnp.sqrt(n2[...] + n3[...] + epsilon)
    new_right[...] = (picked * inverse)[0:5].astype(BF16)
    scaled = ortho * inverse[0:1, :]
    scale = (M * N / R) ** 0.5
    for h in range(2):
        lanes = slice(span * h, span * (h + 1))
        update = triple(scaled, rt[h], NN)
        new_weight[:, lanes] = decay_keep * weight[:, lanes] - step_rate * scale * update[0:rows]
    for copy in sent:
        copy.wait_send()


def copies_of(Y, ZH):
    return 4 + 2 + 2 * (Y - 1) + 2 * 3 + 2 * (ZH - 1) + (Y - 1) + 1 + 2 + 3 + (Y - 1) + 1 + 2


def on_device(dims, weight, grad, momentum, right_factor):
    Y, ZH = dims
    rows, width = weight.shape
    padded = -(-rows // 8) * 8
    span = width // 2
    ry = HALF // Y
    rc = ry // 2
    rg = 64 // Y
    total = copies_of(Y, ZH)
    vm = lambda *shape: pltpu.VMEM(shape, F32)
    scratch = [
        vm(padded, width), vm(2, padded, HALF), vm(2, padded, HALF), vm(4, padded, HALF),
        vm(2, R, span), vm(2, HALF, span), vm(2, HALF, span), vm(Y - 1, 2, ry, span),
        vm(2, ry, span), vm(ZL - 1, rc, span), vm(ZH, rc, span), vm(2, R, span),
        vm(2, R, HALF), vm(64, HALF), vm(64, HALF), vm(Y - 1, rg, HALF),
        vm(ZL, rg, HALF), vm(ZH, rg, HALF), vm(2, R, HALF), vm(HALF, 2 * HALF), vm(R, R),
        vm(2, R, span), vm(8, R), vm(8, R), vm(8, R), vm(8, R),
        pltpu.SemaphoreType.DMA((total,)), pltpu.SemaphoreType.DMA((total,)),
    ]
    vmem = pl.BlockSpec(memory_space=pltpu.VMEM)
    return pl.pallas_call(
        functools.partial(kernel, dims),
        out_shape=(
            jax.ShapeDtypeStruct((rows, width), F32),
            jax.ShapeDtypeStruct((rows, width), F32),
            jax.ShapeDtypeStruct((5, R), BF16),
        ),
        in_specs=[vmem] * 4,
        out_specs=(vmem,) * 3,
        scratch_shapes=scratch,
        compiler_params=pltpu.CompilerParams(
            collective_id=0, has_side_effects=True, vmem_limit_bytes=60 * 1024 * 1024
        ),
        name="dion_step",
    )(weight, grad, momentum, right_factor)


def solution(mesh):
    placed = (P("row", "col"), P("row", "col"), P("row", "col"), P("col", None))
    return jax.shard_map(
        functools.partial(on_device, (8, 4)),
        mesh=mesh,
        in_specs=placed,
        out_specs=(P("row", "col"), P("row", "col"), P(("col", "row"), None)),
        check_vma=False,
    )
```

time: 1110 us -> 104 us (0.09)
  the two profiles are of different devices: /device:TPU:1 before, /device:TPU:66 now
where the time goes in v1:
time: 104 us
  Pallas kernels  100 us (96%)
  local copies, waits for them, and re-layouts  3.33 us (3%)
    pallas_call x1, Pallas kernels, on_device(): pl.pallas_call(functools.partial(kernel, dims), out_shape=(jax.ShapeDtype...  100 us
    unnamed x7, local copies, waits for them, and re-layouts  3.33 us

profile of v1, /device:TPU:66, one launch (start us, length us, event | category | flops | bytes accessed | tf_op | source)
XLA Modules:
  0.0 104.3 jit_solution(1080268585950626476)
XLA Ops:
  0.6 100.3 %dion_step.1 = (f32[100,1280]{1,0:T(8,128)}, f32[100,1280]{1,0:T(8,128)}, bf16[5,256]{1,0:T(8,128)(2,1)}) custom-call(f32[100,1280]{1,0:T(8,128)} %weight.1, f32[100,1280]{1,0:T(8,128)} %grad.1, f32[100,1280]{1,0:T(8,128)} %momentum.1, bf16[1280,256]{1,0:T(8,128)(2,1)} %factor.1), custom_call_target="tpu_custom_call" | custom-call | tf_op jit(solution)/shard_map/dion_step/pallas_call | solution.py:346
  100.9 0.0 copy-start
  100.9 1.9 %copy.10 = f32[100,1280]{1,0:T(8,128)} copy(f32[100,1280]{1,0:T(8,128)} %get-tuple-element.6) | data formatting | bytes 1024000
  102.9 0.0 copy-done
  102.9 0.0 copy-start.1
  102.9 0.8 copy.11
  103.7 0.0 copy-done.1
  103.7 0.6 copy.12
Async XLA Ops:
  100.9 1.9 %copy-start = (f32[100,1280]{1,0:T(8,128)S(1)}, f32[100,1280]{1,0:T(8,128)}, u32[]{:S(2)}) copy-start(f32[100,1280]{1,0:T(8,128)} %get-tuple-element.7) | copy-start | bytes 1536004
  102.9 0.8 copy-start.1

commit v2 on v1

--- a/solution.py
+++ b/solution.py
@@ -52,7 +52,7 @@
     return high, middle, rest - middle
 
 
-def invert_factor(work):
+def invert_factor(work, first, last):
     lane = lax.broadcasted_iota(jnp.int32, (8, HALF), 1)
     sub = lax.broadcasted_iota(jnp.int32, (8, HALF), 0)
 
@@ -89,13 +89,13 @@
         work[...] = work[...] - single(left, right, TN)
         return carry
 
-    lax.fori_loop(0, HALF // 8, group, 0)
+    lax.fori_loop(first, last, group, 0)
 
 
 def kernel(
     dims, weight, grad, momentum, factor, new_weight, new_momentum, new_right,
-    buf, part, both, rx, wt, cw, accw, yw, ysum, zw, hw, full,
-    gp, gc, ga, gy, gz, gh, gfin, work, inv, rt, n0, n1, n2, n3, ssem, rsem,
+    buf, part, both, rx, pr, wt, cw, accw, ring, ysum, zw, hw, full,
+    gp, gc, ga, gy, gz, gh, gfin, work, inv, rt, tiles, nz, ssem, rsem,
 ):
     Y, ZH = dims
     rows = weight.shape[0]
@@ -119,14 +119,19 @@
     near = at(y, z, core, c + 1 - 2 * lax.rem(c, 2))
     far = at(y, z, core, 3 - c)
     twin = at(y, z, 1 - core, c)
+    xdev = [at(y, z, core, lax.rem(c + d, 4)) for d in range(1, 4)]
     ys = [lax.rem(y + d, Y) for d in range(1, Y)]
     zls = [lax.rem(zl + d, ZL) for d in range(1, ZL)]
     zhs = [lax.rem(zh + d, ZH) for d in range(1, ZH)]
     ydev = [at(q, z, core, c) for q in ys]
     zldev = [at(y, zh * ZL + q, core, c) for q in zls]
     zhdev = [at(y, q * ZL + zl, core, c) for q in zhs]
+    up, down = at(lax.rem(y + 1, Y), z, core, c), at(lax.rem(y + Y - 1, Y), z, core, c)
+    hops = {(0, 1): Y // 2, (1, -1): Y // 2, (1, 1): Y // 2 - 1, (0, -1): Y // 2 - 1}
+    ways = [w for w in hops if hops[w]]
 
     count = [0]
+    sent = []
 
     def send(src, dst, device):
         k = count[0]
@@ -139,14 +144,12 @@
         sent.append(copy)
         return copy
 
-    sent = []
-
     def arrive(copies):
         for copy in copies:
             copy.wait_recv()
 
     barrier = pltpu.get_barrier_semaphore()
-    peers = [near, far, twin] + ydev + zldev + zhdev
+    peers = xdev + [twin] + ydev + zldev + zhdev
     for device in peers:
         pl.semaphore_signal(barrier, inc=1, device_id=device, device_id_type=pl.DeviceIdType.MESH)
 
@@ -168,43 +171,90 @@
     both[...] = part[...] + rx[0:2]
     two = [send(both.at[0], rx.at[2], far), send(both.at[1], rx.at[3], near)]
     arrive(two)
-    part0 = both[0] + rx[2]
-    part1 = both[1] + rx[3]
-    proj = jnp.concatenate([part0, part1], axis=1)
+    pr[0] = both[0] + rx[2]
+    pr[1] = both[1] + rx[3]
+    proj = jnp.concatenate([pr[0], pr[1]], axis=1)
 
     gram = exact(proj, proj, TN)
     gp[0] = gram[:, 0:HALF]
     gp[1] = gram[:, HALF:]
     quarter = pl.multiple_of(c * 64, 64)
     gcopy = send(gp.at[1 - core, pl.ds(quarter, 64)], gc, twin)
-    ph, pm = split(proj)
+    mine = pl.multiple_of(core * HALF, HALF)
+    ph, pm = split(pr[1 - core])
+    wcopies = []
     for h in range(2):
         b_h, b_l = split(buf[:, span * h : span * (h + 1)])
         wt[h] = single(ph, b_h, TN) + (single(ph, b_l, TN) + single(pm, b_h, TN))
-    other = pl.multiple_of((1 - core) * HALF, HALF)
-    mine = pl.multiple_of(core * HALF, HALF)
-    wcopy = send(wt.at[:, pl.ds(other, HALF)], cw, twin)
-
+        wcopies.append(send(wt.at[h], cw.at[h], twin))
+    ph, pm = split(pr[core])
+    for h in range(2):
+        b_h, b_l = split(buf[:, span * h : span * (h + 1)])
+        accw[h] = single(ph, b_h, TN) + (single(ph, b_l, TN) + single(pm, b_h, TN))
     arrive([gcopy])
     ga[...] = gp[core, pl.ds(quarter, 64), :] + gc[...]
     gcopies = [
         send(ga.at[pl.ds(pl.multiple_of(q * rg, 8), rg)], gy.at[d], ydev[d]) for d, q in enumerate(ys)
     ]
-    arrive([wcopy])
-    accw[...] = wt[:, pl.ds(mine, HALF), :] + cw[...]
-    wcopies = [
-        send(accw.at[:, pl.ds(pl.multiple_of(q * ry, ry), ry)], yw.at[d], ydev[d])
-        for d, q in enumerate(ys)
-    ]
+
+    def chunk(h, sign, left):
+        q = lax.rem(y + sign * left + Y, Y)
+        return accw.at[h, pl.ds(pl.multiple_of(q * ry, ry), ry)]
+
+    slots = {}
+    for w in ways:
+        for step in range(1, hops[w] + 1):
+            slots[w + (step,)] = len(slots)
+    flying = {}
+
+    def pass_on(w, step):
+        h, sign = w
+        if step > 1:
+            arrive([flying[w]])
+            ref = chunk(h, sign, hops[w] + 1 - step)
+            ref[...] = ref[...] + ring[slots[w + (step - 1,)]]
+        flying[w] = send(
+            chunk(h, sign, hops[w] + 1 - step), ring.at[slots[w + (step,)]], up if sign > 0 else down
+        )
+
+    for h in range(2):
+        arrive([wcopies[h]])
+        accw[h] = accw[h] + cw[h]
+        for w in ways:
+            if w[0] == h:
+                pass_on(w, 1)
+
+    def ring_step(step):
+        for w in ways:
+            if hops[w] >= step:
+                pass_on(w, step)
+
+    ring_step(2)
     arrive(gcopies)
     tile = ga[pl.ds(pl.multiple_of(y * rg, 8), rg), :]
     for d in range(Y - 1):
         tile = tile + gy[d]
     gz[zl] = tile
     gcopies = [send(gz.at[zl], gz.at[zl], device) for device in zldev]
+    ring_step(3)
     arrive(gcopies)
     gh[zh] = (gz[0] + gz[1]) + (gz[2] + gz[3])
     gcopies = [send(gh.at[zh], gh.at[zh], device) for device in zhdev]
+    ring_step(4)
+    own = pl.multiple_of(y * ry, ry)
+    for h in range(2):
+        block = accw[h, pl.ds(own, ry), :]
+        for w in ways:
+            if w[0] == h:
+                arrive([flying[w]])
+                block = block + ring[slots[w + (hops[w],)]]
+        ysum[h] = block
+    wcopies = [
+        send(
+            ysum.at[lax.rem(q, 2), pl.ds(pl.multiple_of((q // 2) * rc, rc), rc)], zw.at[d], zldev[d]
+        )
+        for d, q in enumerate(zls)
+    ]
     arrive(gcopies)
     tile = gh[0]
     for q in range(1, ZH):
@@ -212,32 +262,19 @@
     spot = pl.multiple_of(c * 64 + y * rg, 8)
     gfin[core, pl.ds(spot, rg), :] = tile
     gcopies = [
-        send(gfin.at[core, pl.ds(spot, rg)], gfin.at[core, pl.ds(spot, rg)], device) for device in ydev
+        send(gfin.at[core, pl.ds(spot, rg)], gfin.at[core, pl.ds(spot, rg)], device)
+        for device in ydev
     ]
-
-    arrive(wcopies)
-    block = accw[:, pl.ds(pl.multiple_of(y * ry, ry), ry), :]
-    for d in range(Y - 1):
-        block = block + yw[d]
-    ysum[...] = block
-    wcopies = [
-        send(
-            ysum.at[lax.rem(q, 2), pl.ds(pl.multiple_of((q // 2) * rc, rc), rc)], zw.at[d], zldev[d]
-        )
-        for d, q in enumerate(zls)
-    ]
-    arrive(gcopies)
-    gcopy = send(
-        gfin.at[core, pl.ds(quarter, 64)], gfin.at[core, pl.ds(quarter, 64)], twin
-    )
-    arrive([gcopy])
-    gcopy = send(gfin.at[:, pl.ds(quarter, 64)], gfin.at[:, pl.ds(quarter, 64)], near)
     arrive(wcopies)
     piece = ysum[lax.rem(zl, 2), pl.ds(pl.multiple_of((zl // 2) * rc, rc), rc), :]
     for d in range(ZL - 1):
         piece = piece + zw[d]
     hw[zh] = piece
     wcopies = [send(hw.at[zh], hw.at[zh], device) for device in zhdev]
+    arrive(gcopies)
+    gcopy = send(gfin.at[core, pl.ds(quarter, 64)], gfin.at[core, pl.ds(quarter, 64)], twin)
+    arrive([gcopy])
+    gcopy = send(gfin.at[:, pl.ds(quarter, 64)], gfin.at[:, pl.ds(quarter, 64)], near)
     arrive([gcopy])
     pair = pl.multiple_of((c // 2) * HALF, HALF)
     gcopy = send(gfin.at[:, pl.ds(pair, HALF)], gfin.at[:, pl.ds(pair, HALF)], far)
@@ -251,11 +288,6 @@
     wcopies = [
         send(full.at[hz, pl.ds(spot, rc)], full.at[hz, pl.ds(spot, rc)], device) for device in zldev
     ]
-    arrive(wcopies)
-    strip = pl.multiple_of(core * HALF + y * ry, ry)
-    wcopies = [
-        send(full.at[:, pl.ds(strip, ry)], full.at[:, pl.ds(strip, ry)], device) for device in ydev
-    ]
     arrive([gcopy])
 
     eye = jnp.where(
@@ -266,9 +298,36 @@
     ).astype(F32)
     work[:, 0:HALF] = gfin[0, 0:HALF, :]
     work[:, HALF:] = eye
-    invert_factor(work)
+    invert_factor(work, 0, 5)
     arrive(wcopies)
-    wcopy = send(full.at[:, pl.ds(mine, HALF)], full.at[:, pl.ds(mine, HALF)], twin)
+
+    def strip(h, sign, away):
+        q = lax.rem(y - sign * away + Y, Y)
+        return full.at[h, pl.ds(pl.multiple_of(mine + q * ry, ry), ry)]
+
+    handed = []
+    flying = {}
+
+    def share(w, step):
+        h, sign = w
+        if step > 1:
+            arrive([flying[w]])
+        ref = strip(h, sign, step - 1)
+        if step <= hops[w]:
+            flying[w] = send(ref, ref, up if sign > 0 else down)
+        if step > 1 or w in ((0, 1), (1, -1)):
+            handed.append(send(ref, ref, twin))
+
+    def share_step(step):
+        for w in ways:
+            if hops[w] + 1 >= step:
+                share(w, step)
+
+    share_step(1)
+    invert_factor(work, 5, 10)
+    share_step(2)
+    invert_factor(work, 10, 16)
+    share_step(3)
     top = work[:, HALF:]
     low = exact(gfin[0, HALF:, :], top, NT)
     inv[0:HALF, 0:HALF] = top
@@ -276,38 +335,40 @@
     work[:, 0:HALF] = gfin[1, HALF:, :] - exact(low, low, NT)
     work[:, HALF:] = eye
     cross = exact(low, top, NN)
-    invert_factor(work)
+    share_step(4)
+    invert_factor(work, 0, 5)
+    share_step(5)
+    invert_factor(work, 5, 16)
     last = work[:, HALF:]
     inv[HALF:, 0:HALF] = -exact(last, cross, NN)
     inv[HALF:, HALF:] = last
 
     whole = inv[...]
-    ortho = triple(proj, whole, NT)
-    arrive([wcopy])
-    ones = jnp.ones((8, span), F32)
-    norms = jnp.zeros((8, R), F32)
+    arrive(handed)
+    lanes_sum = jnp.zeros((R, HALF), F32)
     for h in range(2):
         value = triple(whole, full[h], NN)
         rt[h] = value
-        norms = norms + exact(ones, value * value, NT)
-    n0[...] = norms
-    copy = send(n0, n1, near)
-    copies = [copy]
+        for j in range(span // HALF):
+            piece = value[:, HALF * j : HALF * (j + 1)]
+            tiles[(span // HALF) * h + j] = piece
+            lanes_sum = lanes_sum + piece * piece
+    nz[c] = exact(jnp.ones((8, HALF), F32), lanes_sum, NT)
+    copies = [send(nz.at[c], nz.at[c], device) for device in xdev]
+    ortho = triple(proj, whole, NT)
     for h in range(2):
         lanes = slice(span * h, span * (h + 1))
         feedback = triple(ortho, rt[h], NN)
         new_momentum[:, lanes] = buf[0:rows, lanes] - feedback_share * feedback[0:rows]
+    want = 5 * r + lax.broadcasted_iota(jnp.int32, (8, HALF), 0)
+    have = lax.broadcasted_iota(jnp.int32, (8, HALF), 1)
+    spot = (5 * r) // HALF
     picked = jnp.zeros((8, R), F32)
-    for h in range(2):
-        want = 5 * r + lax.broadcasted_iota(jnp.int32, (8, span), 0)
-        have = span * h + lax.broadcasted_iota(jnp.int32, (8, span), 1)
-        chosen = jnp.where(want == have, 1.0, 0.0).astype(F32)
-        picked = picked + exact(chosen, rt[h], NT)
+    for k in range(2):
+        chosen = jnp.where(want == have + HALF * (spot + k), 1.0, 0.0).astype(F32)
+        picked = picked + exact(chosen, tiles[jnp.minimum(spot + k, 2 * span // HALF - 1)], NT)
     arrive(copies)
-    n2[...] = n0[...] + n1[...]
-    copies = [send(n2, n3, far)]
-    arrive(copies)
-    inverse = 1.0 / jnp.sqrt(n2[...] + n3[...] + epsilon)
+    inverse = 1.0 / jnp.sqrt(((nz[0] + nz[1]) + (nz[2] + nz[3])) + epsilon)
     new_right[...] = (picked * inverse)[0:5].astype(BF16)
     scaled = ortho * inverse[0:1, :]
     scale = (M * N / R) ** 0.5
@@ -320,7 +381,7 @@
 
 
 def copies_of(Y, ZH):
-    return 4 + 2 + 2 * (Y - 1) + 2 * 3 + 2 * (ZH - 1) + (Y - 1) + 1 + 2 + 3 + (Y - 1) + 1 + 2
+    return 4 + 1 + 2 + 4 * (Y - 1) + 4 * 3 + 2 * (ZH - 1) + 3 + 3 + 2 * (Y - 1) + 2 * Y + 16
 
 
 def on_device(dims, weight, grad, momentum, right_factor):
@@ -335,11 +396,11 @@
     vm = lambda *shape: pltpu.VMEM(shape, F32)
     scratch = [
         vm(padded, width), vm(2, padded, HALF), vm(2, padded, HALF), vm(4, padded, HALF),
-        vm(2, R, span), vm(2, HALF, span), vm(2, HALF, span), vm(Y - 1, 2, ry, span),
-        vm(2, ry, span), vm(ZL - 1, rc, span), vm(ZH, rc, span), vm(2, R, span),
-        vm(2, R, HALF), vm(64, HALF), vm(64, HALF), vm(Y - 1, rg, HALF),
+        vm(2, padded, HALF), vm(2, HALF, span), vm(2, HALF, span), vm(2, HALF, span),
+        vm(2 * (Y - 1), ry, span), vm(2, ry, span), vm(ZL - 1, rc, span), vm(ZH, rc, span),
+        vm(2, R, span), vm(2, R, HALF), vm(64, HALF), vm(64, HALF), vm(Y - 1, rg, HALF),
         vm(ZL, rg, HALF), vm(ZH, rg, HALF), vm(2, R, HALF), vm(HALF, 2 * HALF), vm(R, R),
-        vm(2, R, span), vm(8, R), vm(8, R), vm(8, R), vm(8, R),
+        vm(2, R, span), vm(width // HALF, R, HALF), vm(4, 8, R),
         pltpu.SemaphoreType.DMA((total,)), pltpu.SemaphoreType.DMA((total,)),
     ]
     vmem = pl.BlockSpec(memory_space=pltpu.VMEM)

time: 104 us -> 94.1 us (0.905)
  the two profiles are of different devices: /device:TPU:66 before, /device:TPU:1 now
where the time goes in v2:
time: 94.1 us; the launch traced here: 92.6 us
  Pallas kernels  88.7 us (94%)
  local copies, waits for them, and re-layouts  3.33 us (4%)
    pallas_call x1, Pallas kernels, on_device(): pl.pallas_call(functools.partial(kernel, dims), out_shape=(jax.ShapeDtype...  88.7 us
    unnamed x7, local copies, waits for them, and re-layouts  3.33 us

profile of v2, /device:TPU:1, one launch (start us, length us, event | category | flops | bytes accessed | tf_op | source)
XLA Modules:
  0.0 92.6 jit_solution(18273699908073124010)
XLA Ops:
  0.6 88.7 %dion_step.1 = (f32[100,1280]{1,0:T(8,128)}, f32[100,1280]{1,0:T(8,128)}, bf16[5,256]{1,0:T(8,128)(2,1)}) custom-call(f32[100,1280]{1,0:T(8,128)} %weight.1, f32[100,1280]{1,0:T(8,128)} %grad.1, f32[100,1280]{1,0:T(8,128)} %momentum.1, bf16[1280,256]{1,0:T(8,128)(2,1)} %factor.1), custom_call_target="tpu_custom_call" | custom-call | tf_op jit(solution)/shard_map/dion_step/pallas_call | solution.py:407
  89.3 0.0 copy-start
  89.3 1.9 %copy.10 = f32[100,1280]{1,0:T(8,128)} copy(f32[100,1280]{1,0:T(8,128)} %get-tuple-element.6) | data formatting | bytes 1024000
  91.2 0.0 copy-done
  91.2 0.0 copy-start.1
  91.2 0.8 copy.11
  92.0 0.0 copy-done.1
  92.0 0.6 copy.12
Async XLA Ops:
  89.3 1.9 %copy-start = (f32[100,1280]{1,0:T(8,128)S(1)}, f32[100,1280]{1,0:T(8,128)}, u32[]{:S(2)}) copy-start(f32[100,1280]{1,0:T(8,128)} %get-tuple-element.7) | copy-start | bytes 1536004
  91.2 0.8 copy-start.1

commit v3 on v2

--- a/solution.py
+++ b/solution.py
@@ -95,7 +95,7 @@
 def kernel(
     dims, weight, grad, momentum, factor, new_weight, new_momentum, new_right,
     buf, part, both, rx, pr, wt, cw, accw, ring, ysum, zw, hw, full,
-    gp, gc, ga, gy, gz, gh, gfin, work, inv, rt, tiles, nz, ssem, rsem,
+    gp, gy, gz, gh, gfin, work, inv, rt, tiles, nz, ssem, rsem,
 ):
     Y, ZH = dims
     rows = weight.shape[0]
@@ -120,10 +120,13 @@
     far = at(y, z, core, 3 - c)
     twin = at(y, z, 1 - core, c)
     xdev = [at(y, z, core, lax.rem(c + d, 4)) for d in range(1, 4)]
-    ys = [lax.rem(y + d, Y) for d in range(1, Y)]
     zls = [lax.rem(zl + d, ZL) for d in range(1, ZL)]
     zhs = [lax.rem(zh + d, ZH) for d in range(1, ZH)]
-    ydev = [at(q, z, core, c) for q in ys]
+    group = [(d, k) for d in range(Y) for k in range(CORES) if d or k]
+    gdev = []
+    for d, k in group:
+        gdev.append((lax.rem(y + d, Y), 1 - core if k else core))
+    gsend = [at(q, z, k, c) for q, k in gdev]
     zldev = [at(y, zh * ZL + q, core, c) for q in zls]
     zhdev = [at(y, q * ZL + zl, core, c) for q in zhs]
     up, down = at(lax.rem(y + 1, Y), z, core, c), at(lax.rem(y + Y - 1, Y), z, core, c)
@@ -149,7 +152,7 @@
             copy.wait_recv()
 
     barrier = pltpu.get_barrier_semaphore()
-    peers = xdev + [twin] + ydev + zldev + zhdev
+    peers = xdev + gsend + zldev + zhdev
     for device in peers:
         pl.semaphore_signal(barrier, inc=1, device_id=device, device_id_type=pl.DeviceIdType.MESH)
 
@@ -175,11 +178,14 @@
     pr[1] = both[1] + rx[3]
     proj = jnp.concatenate([pr[0], pr[1]], axis=1)
 
-    gram = exact(proj, proj, TN)
+    gram = exact(pr[c // 2], proj, TN)
     gp[0] = gram[:, 0:HALF]
     gp[1] = gram[:, HALF:]
-    quarter = pl.multiple_of(c * 64, 64)
-    gcopy = send(gp.at[1 - core, pl.ds(quarter, 64)], gc, twin)
+    inner = lax.rem(c, 2) * 64
+    gcopies = [
+        send(gp.at[k, pl.ds(pl.multiple_of(inner + q * rg, 8), rg)], gy.at[d], gsend[d])
+        for d, (q, k) in enumerate(gdev)
+    ]
     mine = pl.multiple_of(core * HALF, HALF)
     ph, pm = split(pr[1 - core])
     wcopies = []
@@ -191,11 +197,12 @@
     for h in range(2):
         b_h, b_l = split(buf[:, span * h : span * (h + 1)])
         accw[h] = single(ph, b_h, TN) + (single(ph, b_l, TN) + single(pm, b_h, TN))
-    arrive([gcopy])
-    ga[...] = gp[core, pl.ds(quarter, 64), :] + gc[...]
-    gcopies = [
-        send(ga.at[pl.ds(pl.multiple_of(q * rg, 8), rg)], gy.at[d], ydev[d]) for d, q in enumerate(ys)
-    ]
+    arrive(gcopies)
+    tile = gp[core, pl.ds(pl.multiple_of(inner + y * rg, 8), rg), :]
+    for d in range(len(group)):
+        tile = tile + gy[d]
+    gz[zl] = tile
+    gcopies = [send(gz.at[zl], gz.at[zl], device) for device in zldev]
 
     def chunk(h, sign, left):
         q = lax.rem(y + sign * left + Y, Y)
@@ -231,16 +238,20 @@
 
     ring_step(2)
     arrive(gcopies)
-    tile = ga[pl.ds(pl.multiple_of(y * rg, 8), rg), :]
-    for d in range(Y - 1):
-        tile = tile + gy[d]
-    gz[zl] = tile
-    gcopies = [send(gz.at[zl], gz.at[zl], device) for device in zldev]
-    ring_step(3)
-    arrive(gcopies)
     gh[zh] = (gz[0] + gz[1]) + (gz[2] + gz[3])
     gcopies = [send(gh.at[zh], gh.at[zh], device) for device in zhdev]
+    ring_step(3)
     ring_step(4)
+    arrive(gcopies)
+    tile = gh[0]
+    for q in range(1, ZH):
+        tile = tile + gh[q]
+    spot = pl.multiple_of(c * 64 + y * rg, 8)
+    gfin[core, pl.ds(spot, rg), :] = tile
+    gcopies = [
+        send(gfin.at[core, pl.ds(spot, rg)], gfin.at[core, pl.ds(spot, rg)], device)
+        for device in gsend
+    ]
     own = pl.multiple_of(y * ry, ry)
     for h in range(2):
         block = accw[h, pl.ds(own, ry), :]
@@ -256,14 +267,10 @@
         for d, q in enumerate(zls)
     ]
     arrive(gcopies)
-    tile = gh[0]
-    for q in range(1, ZH):
-        tile = tile + gh[q]
-    spot = pl.multiple_of(c * 64 + y * rg, 8)
-    gfin[core, pl.ds(spot, rg), :] = tile
+    quarter = pl.multiple_of(c * 64, 64)
     gcopies = [
-        send(gfin.at[core, pl.ds(spot, rg)], gfin.at[core, pl.ds(spot, rg)], device)
-        for device in ydev
+        send(gfin.at[:, pl.ds(quarter, 64)], gfin.at[:, pl.ds(quarter, 64)], device)
+        for device in xdev
     ]
     arrive(wcopies)
     piece = ysum[lax.rem(zl, 2), pl.ds(pl.multiple_of((zl // 2) * rc, rc), rc), :]
@@ -272,12 +279,37 @@
     hw[zh] = piece
     wcopies = [send(hw.at[zh], hw.at[zh], device) for device in zhdev]
     arrive(gcopies)
-    gcopy = send(gfin.at[core, pl.ds(quarter, 64)], gfin.at[core, pl.ds(quarter, 64)], twin)
-    arrive([gcopy])
-    gcopy = send(gfin.at[:, pl.ds(quarter, 64)], gfin.at[:, pl.ds(quarter, 64)], near)
-    arrive([gcopy])
-    pair = pl.multiple_of((c // 2) * HALF, HALF)
-    gcopy = send(gfin.at[:, pl.ds(pair, HALF)], gfin.at[:, pl.ds(pair, HALF)], far)
+
+    eye = jnp.where(
+        lax.broadcasted_iota(jnp.int32, (HALF, HALF), 0)
+        == lax.broadcasted_iota(jnp.int32, (HALF, HALF), 1),
+        1.0,
+        0.0,
+    ).astype(F32)
+    half_groups = HALF // 8
+    place = [0]
+    kept = []
+
+    def advance(groups):
+        while groups and place[0] < 2 * half_groups:
+            if place[0] == 0:
+                work[:, 0:HALF] = gfin[0, 0:HALF, :]
+                work[:, HALF:] = eye
+            if place[0] == half_groups:
+                top = work[:, HALF:]
+                low = exact(gfin[0, HALF:, :], top, NT)
+                inv[0:HALF, 0:HALF] = top
+                inv[0:HALF, HALF:] = jnp.zeros((HALF, HALF), F32)
+                work[:, 0:HALF] = gfin[1, HALF:, :] - exact(low, low, NT)
+                work[:, HALF:] = eye
+                kept.append(exact(low, top, NN))
+            first = place[0] % half_groups
+            take = min(groups, half_groups - first)
+            invert_factor(work, first, first + take)
+            groups -= take
+            place[0] += take
+
+    advance(8)
     arrive(wcopies)
     piece = hw[0]
     for q in range(1, ZH):
@@ -288,17 +320,7 @@
     wcopies = [
         send(full.at[hz, pl.ds(spot, rc)], full.at[hz, pl.ds(spot, rc)], device) for device in zldev
     ]
-    arrive([gcopy])
-
-    eye = jnp.where(
-        lax.broadcasted_iota(jnp.int32, (HALF, HALF), 0)
-        == lax.broadcasted_iota(jnp.int32, (HALF, HALF), 1),
-        1.0,
-        0.0,
-    ).astype(F32)
-    work[:, 0:HALF] = gfin[0, 0:HALF, :]
-    work[:, HALF:] = eye
-    invert_factor(work, 0, 5)
+    advance(7)
     arrive(wcopies)
 
     def strip(h, sign, away):
@@ -324,23 +346,16 @@
                 share(w, step)
 
     share_step(1)
-    invert_factor(work, 5, 10)
+    advance(3)
     share_step(2)
-    invert_factor(work, 10, 16)
+    advance(5)
     share_step(3)
-    top = work[:, HALF:]
-    low = exact(gfin[0, HALF:, :], top, NT)
-    inv[0:HALF, 0:HALF] = top
-    inv[0:HALF, HALF:] = jnp.zeros((HALF, HALF), F32)
-    work[:, 0:HALF] = gfin[1, HALF:, :] - exact(low, low, NT)
-    work[:, HALF:] = eye
-    cross = exact(low, top, NN)
+    advance(5)
     share_step(4)
-    invert_factor(work, 0, 5)
+    advance(4)
     share_step(5)
-    invert_factor(work, 5, 16)
     last = work[:, HALF:]
-    inv[HALF:, 0:HALF] = -exact(last, cross, NN)
+    inv[HALF:, 0:HALF] = -exact(last, kept[0], NN)
     inv[HALF:, HALF:] = last
 
     whole = inv[...]
@@ -378,10 +393,11 @@
         new_weight[:, lanes] = decay_keep * weight[:, lanes] - step_rate * scale * update[0:rows]
     for copy in sent:
         copy.wait_send()
+    assert count[0] == ssem.shape[0]
 
 
 def copies_of(Y, ZH):
-    return 4 + 1 + 2 + 4 * (Y - 1) + 4 * 3 + 2 * (ZH - 1) + 3 + 3 + 2 * (Y - 1) + 2 * Y + 16
+    return 21 + 2 * (2 * Y - 1) + 2 * (ZH - 1) + 4 * (Y - 1) + 2 * Y
 
 
 def on_device(dims, weight, grad, momentum, right_factor):
@@ -398,7 +414,7 @@
         vm(padded, width), vm(2, padded, HALF), vm(2, padded, HALF), vm(4, padded, HALF),
         vm(2, padded, HALF), vm(2, HALF, span), vm(2, HALF, span), vm(2, HALF, span),
         vm(2 * (Y - 1), ry, span), vm(2, ry, span), vm(ZL - 1, rc, span), vm(ZH, rc, span),
-        vm(2, R, span), vm(2, R, HALF), vm(64, HALF), vm(64, HALF), vm(Y - 1, rg, HALF),
+        vm(2, R, span), vm(2, HALF, HALF), vm(2 * Y - 1, rg, HALF),
         vm(ZL, rg, HALF), vm(ZH, rg, HALF), vm(2, R, HALF), vm(HALF, 2 * HALF), vm(R, R),
         vm(2, R, span), vm(width // HALF, R, HALF), vm(4, 8, R),
         pltpu.SemaphoreType.DMA((total,)), pltpu.SemaphoreType.DMA((total,)),

time: 94.1 us -> 93.4 us (level); the launches traced: 92.6 us -> 93.2 us
  no operation moved by 1% of the time
where the time goes in v3:
time: 93.4 us; the launch traced here: 93.2 us
  Pallas kernels  89.2 us (96%)
  local copies, waits for them, and re-layouts  3.33 us (4%)
    pallas_call x1, Pallas kernels, on_device(): pl.pallas_call(functools.partial(kernel, dims), out_shape=(jax.ShapeDtype...  89.2 us
    unnamed x7, local copies, waits for them, and re-layouts  3.33 us

profile of v3, /device:TPU:1, one launch (start us, length us, event | category | flops | bytes accessed | tf_op | source)
XLA Modules:
  0.0 93.2 jit_solution(4894705956228283113)
XLA Ops:
  0.6 89.2 %dion_step.1 = (f32[100,1280]{1,0:T(8,128)}, f32[100,1280]{1,0:T(8,128)}, bf16[5,256]{1,0:T(8,128)(2,1)}) custom-call(f32[100,1280]{1,0:T(8,128)} %weight.1, f32[100,1280]{1,0:T(8,128)} %grad.1, f32[100,1280]{1,0:T(8,128)} %momentum.1, bf16[1280,256]{1,0:T(8,128)(2,1)} %factor.1), custom_call_target="tpu_custom_call" | custom-call | tf_op jit(solution)/shard_map/dion_step/pallas_call | solution.py:423
  89.9 0.0 copy-start
  89.9 1.9 %copy.10 = f32[100,1280]{1,0:T(8,128)} copy(f32[100,1280]{1,0:T(8,128)} %get-tuple-element.6) | data formatting | bytes 1024000
  91.8 0.0 copy-done
  91.8 0.0 copy-start.1
  91.8 0.8 copy.11
  92.6 0.0 copy-done.1
  92.6 0.6 copy.12
Async XLA Ops:
  89.9 1.9 %copy-start = (f32[100,1280]{1,0:T(8,128)S(1)}, f32[100,1280]{1,0:T(8,128)}, u32[]{:S(2)}) copy-start(f32[100,1280]{1,0:T(8,128)} %get-tuple-element.7) | copy-start | bytes 1536004
  91.8 0.8 copy-start.1

commit v4 on v3

--- a/solution.py
+++ b/solution.py
@@ -19,6 +19,7 @@
 CORES = 2
 ZL = 4
 HALF = 128
+PANEL = 32
 F32 = jnp.float32
 BF16 = jnp.bfloat16
 NN = (((1,), (0,)), ((), ()))
@@ -53,34 +54,33 @@
 
 
 def invert_factor(work, first, last):
-    lane = lax.broadcasted_iota(jnp.int32, (8, HALF), 1)
-    sub = lax.broadcasted_iota(jnp.int32, (8, HALF), 0)
+    lane = lax.broadcasted_iota(jnp.int32, (PANEL, HALF), 1)
+    sub = lax.broadcasted_iota(jnp.int32, (PANEL, HALF), 0)
 
     def group(g, carry):
-        base = pl.multiple_of(g * 8, 8)
-        ra = work[pl.ds(base, 8), 0:HALF]
-        rb = work[pl.ds(base, 8), HALF:]
+        base = pl.multiple_of(g * PANEL, PANEL)
+        ra = work[pl.ds(base, PANEL), 0:HALF]
+        rb = work[pl.ds(base, PANEL), HALF:]
         columns = [
             jnp.broadcast_to(
-                jnp.sum(jnp.where(lane == base + i, ra, 0.0), axis=1, keepdims=True), (8, HALF)
+                jnp.sum(jnp.where(lane == base + i, ra, 0.0), axis=1, keepdims=True), (PANEL, HALF)
             )
-            for i in range(8)
+            for i in range(PANEL)
         ]
-        for i in range(8):
-            pivot = jnp.broadcast_to(columns[i][i : i + 1, :], (8, HALF))
+        for i in range(PANEL):
+            pivot = jnp.broadcast_to(columns[i][i : i + 1, :], (PANEL, HALF))
             s = lax.rsqrt(pivot)
-            s = s * (1.5 - 0.5 * pivot * s * s)
             scaled = columns[i] * s
             below = jnp.where(sub > i, scaled, 0.0)
-            for j in range(i + 1, 8):
-                columns[j] = columns[j] - below * jnp.broadcast_to(scaled[j : j + 1, :], (8, HALF))
-            pa = jnp.broadcast_to(ra[i : i + 1, :], (8, HALF)) * s
-            pb = jnp.broadcast_to(rb[i : i + 1, :], (8, HALF)) * s
+            for j in range(i + 1, PANEL):
+                columns[j] = columns[j] - below * jnp.broadcast_to(scaled[j : j + 1, :], (PANEL, HALF))
+            pa = jnp.broadcast_to(ra[i : i + 1, :], (PANEL, HALF)) * s
+            pb = jnp.broadcast_to(rb[i : i + 1, :], (PANEL, HALF)) * s
             ra = jnp.where(sub == i, pa, ra - below * pa)
             rb = jnp.where(sub == i, pb, rb - below * pb)
-        work[pl.ds(base, 8), 0:HALF] = ra
-        work[pl.ds(base, 8), HALF:] = rb
-        masked = jnp.where(lane >= base + 8, ra, 0.0)
+        work[pl.ds(base, PANEL), 0:HALF] = ra
+        work[pl.ds(base, PANEL), HALF:] = rb
+        masked = jnp.where(lane >= base + PANEL, ra, 0.0)
         lh, lm, ll = thirds(masked)
         full = jnp.concatenate([ra, rb], axis=1)
         rh, rm, rl = thirds(full)
@@ -242,16 +242,6 @@
     gcopies = [send(gh.at[zh], gh.at[zh], device) for device in zhdev]
     ring_step(3)
     ring_step(4)
-    arrive(gcopies)
-    tile = gh[0]
-    for q in range(1, ZH):
-        tile = tile + gh[q]
-    spot = pl.multiple_of(c * 64 + y * rg, 8)
-    gfin[core, pl.ds(spot, rg), :] = tile
-    gcopies = [
-        send(gfin.at[core, pl.ds(spot, rg)], gfin.at[core, pl.ds(spot, rg)], device)
-        for device in gsend
-    ]
     own = pl.multiple_of(y * ry, ry)
     for h in range(2):
         block = accw[h, pl.ds(own, ry), :]
@@ -267,10 +257,14 @@
         for d, q in enumerate(zls)
     ]
     arrive(gcopies)
-    quarter = pl.multiple_of(c * 64, 64)
+    tile = gh[0]
+    for q in range(1, ZH):
+        tile = tile + gh[q]
+    spot = pl.multiple_of(c * 64 + y * rg, 8)
+    gfin[core, pl.ds(spot, rg), :] = tile
     gcopies = [
-        send(gfin.at[:, pl.ds(quarter, 64)], gfin.at[:, pl.ds(quarter, 64)], device)
-        for device in xdev
+        send(gfin.at[core, pl.ds(spot, rg)], gfin.at[core, pl.ds(spot, rg)], device)
+        for device in gsend
     ]
     arrive(wcopies)
     piece = ysum[lax.rem(zl, 2), pl.ds(pl.multiple_of((zl // 2) * rc, rc), rc), :]
@@ -279,6 +273,11 @@
     hw[zh] = piece
     wcopies = [send(hw.at[zh], hw.at[zh], device) for device in zhdev]
     arrive(gcopies)
+    quarter = pl.multiple_of(c * 64, 64)
+    gcopies = [
+        send(gfin.at[:, pl.ds(quarter, 64)], gfin.at[:, pl.ds(quarter, 64)], device)
+        for device in xdev
+    ]
 
     eye = jnp.where(
         lax.broadcasted_iota(jnp.int32, (HALF, HALF), 0)
@@ -286,7 +285,7 @@
         1.0,
         0.0,
     ).astype(F32)
-    half_groups = HALF // 8
+    half_groups = HALF // PANEL
     place = [0]
     kept = []
 
@@ -309,7 +308,6 @@
             groups -= take
             place[0] += take
 
-    advance(8)
     arrive(wcopies)
     piece = hw[0]
     for q in range(1, ZH):
@@ -320,7 +318,8 @@
     wcopies = [
         send(full.at[hz, pl.ds(spot, rc)], full.at[hz, pl.ds(spot, rc)], device) for device in zldev
     ]
-    advance(7)
+    arrive(gcopies)
+    advance(2)
     arrive(wcopies)
 
     def strip(h, sign, away):
@@ -346,13 +345,13 @@
                 share(w, step)
 
     share_step(1)
-    advance(3)
+    advance(2)
     share_step(2)
-    advance(5)
+    advance(1)
     share_step(3)
-    advance(5)
+    advance(1)
     share_step(4)
-    advance(4)
+    advance(2)
     share_step(5)
     last = work[:, HALF:]
     inv[HALF:, 0:HALF] = -exact(last, kept[0], NN)

time: 93.4 us -> 92.9 us (level)
  no operation moved by 1% of the time
where the time goes in v4:
time: 92.9 us; the launch traced here: 92.7 us
  Pallas kernels  88.7 us (95%)
  local copies, waits for them, and re-layouts  3.33 us (4%)
    pallas_call x1, Pallas kernels, on_device(): pl.pallas_call(functools.partial(kernel, dims), out_shape=(jax.ShapeDtype...  88.7 us
    unnamed x7, local copies, waits for them, and re-layouts  3.33 us

profile of v4, /device:TPU:1, one launch (start us, length us, event | category | flops | bytes accessed | tf_op | source)
XLA Modules:
  0.0 92.7 jit_solution(15491869652525552188)
XLA Ops:
  0.6 88.7 %dion_step.1 = (f32[100,1280]{1,0:T(8,128)}, f32[100,1280]{1,0:T(8,128)}, bf16[5,256]{1,0:T(8,128)(2,1)}) custom-call(f32[100,1280]{1,0:T(8,128)} %weight.1, f32[100,1280]{1,0:T(8,128)} %grad.1, f32[100,1280]{1,0:T(8,128)} %momentum.1, bf16[1280,256]{1,0:T(8,128)(2,1)} %factor.1), custom_call_target="tpu_custom_call" | custom-call | tf_op jit(solution)/shard_map/dion_step/pallas_call | solution.py:422
  89.3 0.0 copy-start
  89.4 1.9 %copy.10 = f32[100,1280]{1,0:T(8,128)} copy(f32[100,1280]{1,0:T(8,128)} %get-tuple-element.6) | data formatting | bytes 1024000
  91.3 0.0 copy-done
  91.3 0.0 copy-start.1
  91.3 0.8 copy.11
  92.1 0.0 copy-done.1
  92.1 0.6 copy.12
Async XLA Ops:
  89.3 1.9 %copy-start = (f32[100,1280]{1,0:T(8,128)S(1)}, f32[100,1280]{1,0:T(8,128)}, u32[]{:S(2)}) copy-start(f32[100,1280]{1,0:T(8,128)} %get-tuple-element.7) | copy-start | bytes 1536004
  91.3 0.8 copy-start.1

commit v5 on v4

--- a/solution.py
+++ b/solution.py
@@ -318,8 +318,6 @@
     wcopies = [
         send(full.at[hz, pl.ds(spot, rc)], full.at[hz, pl.ds(spot, rc)], device) for device in zldev
     ]
-    arrive(gcopies)
-    advance(2)
     arrive(wcopies)
 
     def strip(h, sign, away):
@@ -345,13 +343,14 @@
                 share(w, step)
 
     share_step(1)
+    arrive(gcopies)
+    advance(3)
+    share_step(2)
     advance(2)
-    share_step(2)
+    share_step(3)
+    advance(2)
+    share_step(4)
     advance(1)
-    share_step(3)
-    advance(1)
-    share_step(4)
-    advance(2)
     share_step(5)
     last = work[:, HALF:]
     inv[HALF:, 0:HALF] = -exact(last, kept[0], NN)

time: 92.9 us -> 92.9 us (level)
  no operation moved by 1% of the time
where the time goes in v5:
time: 92.9 us; the launch traced here: 92.7 us
  Pallas kernels  88.8 us (96%)
  local copies, waits for them, and re-layouts  3.33 us (4%)
    pallas_call x1, Pallas kernels, on_device(): pl.pallas_call(functools.partial(kernel, dims), out_shape=(jax.ShapeDtype...  88.8 us
    unnamed x7, local copies, waits for them, and re-layouts  3.33 us

profile of v5, /device:TPU:1, one launch (start us, length us, event | category | flops | bytes accessed | tf_op | source)
XLA Modules:
  0.0 92.7 jit_solution(4374044789228272786)
XLA Ops:
  0.6 88.8 %dion_step.1 = (f32[100,1280]{1,0:T(8,128)}, f32[100,1280]{1,0:T(8,128)}, bf16[5,256]{1,0:T(8,128)(2,1)}) custom-call(f32[100,1280]{1,0:T(8,128)} %weight.1, f32[100,1280]{1,0:T(8,128)} %grad.1, f32[100,1280]{1,0:T(8,128)} %momentum.1, bf16[1280,256]{1,0:T(8,128)(2,1)} %factor.1), custom_call_target="tpu_custom_call" | custom-call | tf_op jit(solution)/shard_map/dion_step/pallas_call | solution.py:421
  89.4 0.0 copy-start
  89.4 1.9 %copy.10 = f32[100,1280]{1,0:T(8,128)} copy(f32[100,1280]{1,0:T(8,128)} %get-tuple-element.6) | data formatting | bytes 1024000
  91.3 0.0 copy-done
  91.4 0.0 copy-start.1
  91.4 0.8 copy.11
  92.2 0.0 copy-done.1
  92.2 0.6 copy.12
Async XLA Ops:
  89.4 1.9 %copy-start = (f32[100,1280]{1,0:T(8,128)S(1)}, f32[100,1280]{1,0:T(8,128)}, u32[]{:S(2)}) copy-start(f32[100,1280]{1,0:T(8,128)} %get-tuple-element.7) | copy-start | bytes 1536004
  91.4 0.8 copy-start.1
